TPU v7x, 512 devices: a whole 4x8x8 slice. The times are simulated.
512 devices in a mesh: section: 16 (over z, core), tensor: 32 (over y, x).
Axes of the slice: x: 4, y: 8, z: 8, core: 2. Of those that a mesh axis runs over, the one named last changes fastest.
Arguments:
- acts_prev: bfloat16 [8192, 8192], P('section', 'tensor'), may hold values from -6 to 6
- embedded: bfloat16 [512, 8192], P(None, 'tensor'), may hold values from -6 to 6
- grads_next: bfloat16 [8192, 8192], P('section', 'tensor'), may hold values from -1.5 to 1.5
- loss_grad: bfloat16 [512, 8192], P(None, 'tensor'), may hold values from -1.5 to 1.5
- up_weight: bfloat16 [16, 2, 256, 32768], P('section', None, None, 'tensor'), may hold values from -0.25 to 0.25
- down_weight: bfloat16 [16, 2, 32768, 256], P('section', None, 'tensor'), may hold values from -0.125 to 0.125
Outputs:
- mixed: bfloat16 [8192, 8192], P('section', 'tensor')
- input_grads: bfloat16 [8192, 8192], P('section', 'tensor')
- up_grad: bfloat16 [16, 2, 256, 32768], P('section', None, None, 'tensor')
- down_grad: bfloat16 [16, 2, 32768, 256], P('section', None, 'tensor')
All inputs are finite; a program needn't handle non-finite values.
Results may differ from a plain program's by a relative error of at most 0.005.
Values may be sent and summed in bfloat16 or wider, within the bound.
A program may use at most 64 MiB of HBM per device.

v0:
```python
import jax
import jax.numpy as jnp
from jax import lax
from jax.sharding import PartitionSpec as P


def from_behind(value, axis, by):
    length = lax.axis_size(axis)
    pairs = [(i, i + by) for i in range(length) if 0 <= i + by < length]
    return lax.ppermute(value, axis, pairs)


def swapped(value, axis, distance):
    mask = 2**distance
    pairs = [(source, source ^ mask) for source in range(lax.axis_size(axis))]
    return lax.ppermute(value, axis, pairs)


def gelu_tanh(values):
    return jax.nn.gelu(values, approximate=True)


def on_device(acts_prev, embedded, grads_next, loss_grad, up_weight, down_weight):
    sections = lax.axis_size("section")
    section_idx = lax.axis_index("section")
    received = from_behind(acts_prev, "section", 1)
    inputs = jnp.where(section_idx == 0, embedded, received)
    returned = from_behind(grads_next, "section", -1)
    cotangent = jnp.where(section_idx == sections - 1, loss_grad, returned)
    up_local = up_weight[0]
    down_local = down_weight[0]
    factors = up_local.shape[0]
    levels = factors - 1
    block_width = up_local.shape[1]
    tokens = inputs.shape[0]
    model_local = inputs.shape[1] // block_width
    hidden_local = up_local.shape[2] // block_width
    expand = hidden_local // model_local
    top_bit = lax.axis_size("tensor").bit_length() - 1
    first_bit = top_bit - levels
    position = 0
    got_inputs, got_grads = swapped((inputs, cotangent), "tensor", first_bit + position)
    their_inputs = [got_inputs]
    their_grads = [got_grads]
    up_shaped = up_local.reshape(factors, block_width, model_local, expand, block_width)
    down_shaped = down_local.reshape(factors, model_local, expand, block_width, block_width)
    stacked_inputs = jnp.stack([inputs] + their_inputs).reshape(
        factors, tokens, model_local, block_width
    )
    pre_act = jnp.einsum(
        "ktmp,kpmeq->tmeq", stacked_inputs, up_shaped, preferred_element_type=jnp.float32
    )
    hidden = gelu_tanh(pre_act).astype(jnp.bfloat16)
    partial_out = jnp.einsum(
        "tmep,kmepq->ktmq", hidden, down_shaped, preferred_element_type=jnp.float32
    )
    out_sum = partial_out[0]
    position = 0
    arrived = swapped(
        partial_out[1 + position].astype(jnp.bfloat16), "tensor", first_bit + position
    )
    out_sum = out_sum + arrived.astype(jnp.float32)
    stacked_grads = jnp.stack([cotangent] + their_grads).reshape(
        factors, tokens, model_local, block_width
    )
    grad_hidden = jnp.einsum(
        "ktmq,kmepq->tmep", stacked_grads, down_shaped, preferred_element_type=jnp.float32
    )
    down_grad_bits = jnp.einsum(
        "tmep,ktmq->kmepq", hidden, stacked_grads, preferred_element_type=jnp.float32
    )
    pullback = jax.vjp(gelu_tanh, pre_act)[1]
    grad_pre = pullback(grad_hidden)[0].astype(jnp.bfloat16)
    up_grad_bits = jnp.einsum(
        "ktmp,tmeq->kpmeq", stacked_inputs, grad_pre, preferred_element_type=jnp.float32
    )
    partial_back = jnp.einsum(
        "tmeq,kpmeq->ktmp", grad_pre, up_shaped, preferred_element_type=jnp.float32
    )
    back_sum = partial_back[0]
    position = 0
    arrived = swapped(
        partial_back[1 + position].astype(jnp.bfloat16), "tensor", first_bit + position
    )
    back_sum = back_sum + arrived.astype(jnp.float32)
    mixed = (
        inputs.astype(jnp.float32) + out_sum.reshape(tokens, model_local * block_width)
    ).astype(jnp.bfloat16)
    input_grads = (
        cotangent.astype(jnp.float32) + back_sum.reshape(tokens, model_local * block_width)
    ).astype(jnp.bfloat16)
    up_grad = up_grad_bits.reshape(factors, block_width, hidden_local * block_width).astype(
        jnp.bfloat16
    )[None]
    down_grad = down_grad_bits.reshape(factors, hidden_local * block_width, block_width).astype(
        jnp.bfloat16
    )[None]
    return (mixed, input_grads, up_grad, down_grad)


def solution(mesh):
    in_specs = (
        P("section", "tensor"),
        P(None, "tensor"),
        P("section", "tensor"),
        P(None, "tensor"),
        P("section", None, None, "tensor"),
        P("section", None, "tensor", None),
    )
    out_specs = (
        P("section", "tensor"),
        P("section", "tensor"),
        P("section", None, None, "tensor"),
        P("section", None, "tensor", None),
    )
    return jax.shard_map(
        on_device, mesh=mesh, in_specs=in_specs, out_specs=out_specs, check_vma=False
    )
```

profile of v0, /device:TPU:196, one launch (start us, length us, event | category | flops | bytes accessed | tf_op | source)
XLA Modules:
  0.0 79.3 jit_solution(2880692884604943334)
XLA Ops:
  0.6 0.0 copy-start
  0.6 0.0 copy-start.3
  0.7 2.1 %collective-permute-start = (bf16[512,256]{1,0:T(8,128)(2,1)}, bf16[512,256]{1,0:T(8,128)(2,1)S(1)}, u32[]{:S(2)}, u32[]{:S(2)}) collective-permute-start(bf16[512,256]{1,0:T(8,128)(2,1)} %param.6), channel_id=1, source_target_pairs={{0,32},{32,64},{64,96},{96,128},{128,160},{160,192},{192,224},{224... | collective-permute-start | bytes 786440 | tf_op jit(solution)/shard_map/ppermute | solution.py:10
  2.7 3.6 %collective-permute-start.3 = (bf16[512,256]{1,0:T(8,128)(2,1)}, bf16[512,256]{1,0:T(8,128)(2,1)S(1)}, u32[]{:S(2)}, u32[]{:S(2)}) collective-permute-start(bf16[512,256]{1,0:T(8,128)(2,1)} %param.8), channel_id=1, source_target_pairs={{32,0},{64,32},{96,64},{128,96},{160,128},{192,160},{224,192},{256... | collective-permute-start | bytes 786440 | tf_op jit(solution)/shard_map/ppermute | solution.py:10
  6.4 2.3 %collective-permute-done = bf16[512,256]{1,0:T(8,128)(2,1)S(1)} collective-permute-done((bf16[512,256]{1,0:T(8,128)(2,1)}, bf16[512,256]{1,0:T(8,128)(2,1)S(1)}, u32[]{:S(2)}, u32[]{:S(2)}) %collective-permute-start) | collective-permute-done | bytes 262176 | tf_op jit(solution)/shard_map/ppermute | solution.py:10
  8.7 7.7 %collective-permute-start.1 = (bf16[512,256]{1,0:T(8,128)(2,1)S(1)}, bf16[512,256]{1,0:T(8,128)(2,1)S(1)}, u32[]{:S(2)}, u32[]{:S(2)}) collective-permute-start(bf16[512,256]{1,0:T(8,128)(2,1)S(1)} %broadcast_select_fusion.1), channel_id=1, source_target_pairs={{0,16},{1,17},{2,18},{3,19},{4,20},{5,21},{6,22},{7,23},{8,24},{9,... | collective-permute-start | bytes 786440 | tf_op jit(solution)/shard_map/ppermute | solution.py:16
  16.5 1.9 %reshape.102 = bf16[2,256,4,256]{3,2,1,0:T(4,128)(2,1)S(1)} reshape(bf16[1,2,256,1024]{3,2,1,0:T(8,128)(2,1)} %param.10) | data formatting | bytes 2097152 | tf_op jit(solution)/shard_map/reshape
  18.3 0.0 collective-permute-done.3
  18.3 0.0 copy-done.3
  18.4 2.0 %collective-permute-start.4 = (bf16[512,256]{1,0:T(8,128)(2,1)S(1)}, bf16[512,256]{1,0:T(8,128)(2,1)S(1)}, u32[]{:S(2)}, u32[]{:S(2)}) collective-permute-start(bf16[512,256]{1,0:T(8,128)(2,1)S(1)} %broadcast_select_fusion), channel_id=1, source_target_pairs={{0,16},{1,17},{2,18},{3,19},{4,20},{5,21},{6,22},{7,23},{8,24},{9,... | collective-permute-start | bytes 786440 | tf_op jit(solution)/shard_map/ppermute | solution.py:16
  20.4 4.6 %collective-permute-done.1 = bf16[512,256]{1,0:T(8,128)(2,1)S(1)} collective-permute-done((bf16[512,256]{1,0:T(8,128)(2,1)S(1)}, bf16[512,256]{1,0:T(8,128)(2,1)S(1)}, u32[]{:S(2)}, u32[]{:S(2)}) %collective-permute-start.1) | collective-permute-done | bytes 262176 | tf_op jit(solution)/shard_map/ppermute | solution.py:16
  25.1 0.7 fusion.17
  25.8 0.0 copy-done
  25.8 0.8 %convolution_bitcast_fusion.1 = f32[2,512,1,256]{3,1,2,0:T(8,128)S(1)} fusion(bf16[2,4,256,256]{3,2,1,0:T(8,128)(2,1)S(1)} %bitcast.152, f32[512,4,256,1]{2,0,3,1:T(8,128)S(1)} %fusion.17), kind=kOutput, calls=%fused_computation.19 | convolution fusion | flops 541589504 | bytes 4194304 | tf_op jit(solution)/shard_map/tmep,kmepq->ktmq/dot_general | solution.py:54
  26.6 14.4 %collective-permute-done.4 = bf16[512,256]{1,0:T(8,128)(2,1)S(1)} collective-permute-done((bf16[512,256]{1,0:T(8,128)(2,1)S(1)}, bf16[512,256]{1,0:T(8,128)(2,1)S(1)}, u32[]{:S(2)}, u32[]{:S(2)}) %collective-permute-start.4) | collective-permute-done | bytes 262176 | tf_op jit(solution)/shard_map/ppermute | solution.py:16
  41.0 1.8 %fusion.6 = bf16[512,1,4,256]{3,0,2,1:T(8,128)(2,1)S(1)} fusion(f32[512,4,256,1]{2,0,3,1:T(8,128)S(1)} %fusion.17, bf16[2,4,256,256]{3,2,1,0:T(8,128)(2,1)S(1)} %bitcast.153, bf16[1,512,256]{2,1,0:T(8,128)(2,1)S(1)} %bitcast.161, bf16[1,512,256]{2,1,0:T(8,128)(2,1)S(1)} %bitcast.157), kind=kOutput, calls=%fused_computation.8 | convolution fusion | flops 548405248 | bytes 4718592 | tf_op jit(solution)/shard_map/ktmq,kmepq->tmep/dot_general | solution.py:66
  42.7 1.9 %convolution_convert_fusion = bf16[2,256,4,256]{1,3,2,0:T(8,128)(2,1)} fusion(bf16[1,512,256]{2,1,0:T(8,128)(2,1)S(1)} %bitcast.162, bf16[1,512,256]{2,1,0:T(8,128)(2,1)S(1)} %bitcast.158, f32[512,4,256,1]{2,0,3,1:T(8,128)S(1)} %fusion.17), kind=kOutput, calls=%fused_computation.16 | convolution fusion | flops 543162368 | bytes 3670016 | tf_op jit(solution)/shard_map/tmep,ktmq->kmepq/dot_general | solution.py:69
  44.7 0.7 convolution_bitcast_fusion
  45.4 0.0 copy-start.2
  45.4 0.8 %fusion.30 = bf16[512,1,256]{2,0,1:T(8,128)(2,1)} fusion(f32[2,512,1,256]{3,1,2,0:T(8,128)S(1)} %convolution_bitcast_fusion), kind=kLoop, calls=%fused_computation.45 | loop fusion | bytes 524288 | tf_op jit(solution)/shard_map/convert_element_type | solution.py:83
  46.2 7.1 %collective-permute-start.5 = (bf16[512,1,256]{2,0,1:T(8,128)(2,1)}, bf16[512,1,256]{2,0,1:T(8,128)(2,1)S(1)}, u32[]{:S(2)}, u32[]{:S(2)}) collective-permute-start(bf16[512,1,256]{2,0,1:T(8,128)(2,1)} %fusion.30), channel_id=1, source_target_pairs={{0,16},{1,17},{2,18},{3,19},{4,20},{5,21},{6,22},{7,23},{8,24},{9,... | collective-permute-start | bytes 786440 | tf_op jit(solution)/shard_map/ppermute | solution.py:16
  53.3 0.0 copy-done.1
  53.3 0.7 fusion.29
  54.0 0.0 copy-done.2
  54.0 2.7 %collective-permute-start.2 = (bf16[512,1,256]{2,0,1:T(8,128)(2,1)}, bf16[512,1,256]{2,0,1:T(8,128)(2,1)S(1)}, u32[]{:S(2)}, u32[]{:S(2)}) collective-permute-start(bf16[512,1,256]{2,0,1:T(8,128)(2,1)} %fusion.29), channel_id=1, source_target_pairs={{0,16},{1,17},{2,18},{3,19},{4,20},{5,21},{6,22},{7,23},{8,24},{9,... | collective-permute-start | bytes 786440 | tf_op jit(solution)/shard_map/ppermute | solution.py:16
  56.7 0.7 fusion.11
  57.5 0.1 copy.19
  57.5 1.3 %copy.21 = bf16[1,2,256,1024]{3,2,1,0:T(8,128)(2,1)} copy(bf16[1,2,256,1024]{2,3,1,0:T(8,128)(2,1)S(1)} %bitcast.154) | data formatting | bytes 2097152
  58.9 13.9 %collective-permute-done.5 = bf16[512,1,256]{2,0,1:T(8,128)(2,1)S(1)} collective-permute-done((bf16[512,1,256]{2,0,1:T(8,128)(2,1)}, bf16[512,1,256]{2,0,1:T(8,128)(2,1)S(1)}, u32[]{:S(2)}, u32[]{:S(2)}) %collective-permute-start.5) | collective-permute-done | bytes 262176 | tf_op jit(solution)/shard_map/ppermute | solution.py:16
  72.8 1.8 %fusion.22 = bf16[512,256]{1,0:T(8,128)(2,1)} fusion(f32[2,512,1,256]{3,1,2,0:T(8,128)} %copy-done.2, bf16[512,1,256]{2,0,1:T(8,128)(2,1)S(1)} %collective-permute-done.5, bf16[512,256]{1,0:T(8,128)(2,1)S(1)} %broadcast_select_fusion), kind=kLoop, calls=%fused_computation.33 | loop fusion | flops 655360 | bytes 1310720 | tf_op jit(solution)/shard_map/convert_element_type | solution.py:91
  74.6 2.9 %collective-permute-done.2 = bf16[512,1,256]{2,0,1:T(8,128)(2,1)S(1)} collective-permute-done((bf16[512,1,256]{2,0,1:T(8,128)(2,1)}, bf16[512,1,256]{2,0,1:T(8,128)(2,1)S(1)}, u32[]{:S(2)}, u32[]{:S(2)}) %collective-permute-start.2) | collective-permute-done | bytes 262176 | tf_op jit(solution)/shard_map/ppermute | solution.py:16
  77.5 1.8 %fusion.26 = bf16[512,256]{1,0:T(8,128)(2,1)} fusion(f32[2,512,1,256]{3,1,2,0:T(8,128)} %copy-done.1, bf16[512,1,256]{2,0,1:T(8,128)(2,1)S(1)} %collective-permute-done.2, bf16[512,256]{1,0:T(8,128)(2,1)S(1)} %broadcast_select_fusion.1), kind=kLoop, calls=%fused_computation.39 | loop fusion | flops 655360 | bytes 1310720 | tf_op jit(solution)/shard_map/convert_element_type | solution.py:88
  (3 shorter events, 0.1 us)
Async XLA Ops:
  0.6 25.1 %copy-start = (bf16[1,2,1024,256]{3,2,1,0:T(8,128)(2,1)S(1)}, bf16[1,2,1024,256]{3,2,1,0:T(8,128)(2,1)}, u32[]{:S(2)}) copy-start(bf16[1,2,1024,256]{3,2,1,0:T(8,128)(2,1)} %param.11) | copy-start | bytes 3145732
  0.6 17.7 %copy-start.3 = (bf16[512,256]{1,0:T(8,128)(2,1)S(1)}, bf16[512,256]{1,0:T(8,128)(2,1)}, u32[]{:S(2)}) copy-start(bf16[512,256]{1,0:T(8,128)(2,1)} %param.9) | copy-start | bytes 786436
  0.7 8.0 %collective-permute-start = (bf16[512,256]{1,0:T(8,128)(2,1)}, bf16[512,256]{1,0:T(8,128)(2,1)S(1)}, u32[]{:S(2)}, u32[]{:S(2)}) collective-permute-start(bf16[512,256]{1,0:T(8,128)(2,1)} %param.6), channel_id=1, source_target_pairs={{0,32},{32,64},{64,96},{96,128},{128,160},{160,192},{192,224},{224... | collective-permute-start | bytes 786440 | tf_op jit(solution)/shard_map/ppermute | solution.py:10
  2.7 15.6 %collective-permute-start.3 = (bf16[512,256]{1,0:T(8,128)(2,1)}, bf16[512,256]{1,0:T(8,128)(2,1)S(1)}, u32[]{:S(2)}, u32[]{:S(2)}) collective-permute-start(bf16[512,256]{1,0:T(8,128)(2,1)} %param.8), channel_id=1, source_target_pairs={{32,0},{64,32},{96,64},{128,96},{160,128},{192,160},{224,192},{256... | collective-permute-start | bytes 786440 | tf_op jit(solution)/shard_map/ppermute | solution.py:10
  8.7 16.3 %collective-permute-start.1 = (bf16[512,256]{1,0:T(8,128)(2,1)S(1)}, bf16[512,256]{1,0:T(8,128)(2,1)S(1)}, u32[]{:S(2)}, u32[]{:S(2)}) collective-permute-start(bf16[512,256]{1,0:T(8,128)(2,1)S(1)} %broadcast_select_fusion.1), channel_id=1, source_target_pairs={{0,16},{1,17},{2,18},{3,19},{4,20},{5,21},{6,22},{7,23},{8,24},{9,... | collective-permute-start | bytes 786440 | tf_op jit(solution)/shard_map/ppermute | solution.py:16
  18.4 22.6 %collective-permute-start.4 = (bf16[512,256]{1,0:T(8,128)(2,1)S(1)}, bf16[512,256]{1,0:T(8,128)(2,1)S(1)}, u32[]{:S(2)}, u32[]{:S(2)}) collective-permute-start(bf16[512,256]{1,0:T(8,128)(2,1)S(1)} %broadcast_select_fusion), channel_id=1, source_target_pairs={{0,16},{1,17},{2,18},{3,19},{4,20},{5,21},{6,22},{7,23},{8,24},{9,... | collective-permute-start | bytes 786440 | tf_op jit(solution)/shard_map/ppermute | solution.py:16
  26.6 26.7 %copy-start.1 = (f32[2,512,1,256]{3,1,2,0:T(8,128)}, f32[2,512,1,256]{3,1,2,0:T(8,128)S(1)}, u32[]{:S(2)}) copy-start(f32[2,512,1,256]{3,1,2,0:T(8,128)S(1)} %convolution_bitcast_fusion.1) | copy-start | bytes 3145732
  45.4 8.6 %copy-start.2 = (f32[2,512,1,256]{3,1,2,0:T(8,128)}, f32[2,512,1,256]{3,1,2,0:T(8,128)S(1)}, u32[]{:S(2)}) copy-start(f32[2,512,1,256]{3,1,2,0:T(8,128)S(1)} %convolution_bitcast_fusion) | copy-start | bytes 3145732
  46.2 26.5 %collective-permute-start.5 = (bf16[512,1,256]{2,0,1:T(8,128)(2,1)}, bf16[512,1,256]{2,0,1:T(8,128)(2,1)S(1)}, u32[]{:S(2)}, u32[]{:S(2)}) collective-permute-start(bf16[512,1,256]{2,0,1:T(8,128)(2,1)} %fusion.30), channel_id=1, source_target_pairs={{0,16},{1,17},{2,18},{3,19},{4,20},{5,21},{6,22},{7,23},{8,24},{9,... | collective-permute-start | bytes 786440 | tf_op jit(solution)/shard_map/ppermute | solution.py:16
  54.0 23.4 %collective-permute-start.2 = (bf16[512,1,256]{2,0,1:T(8,128)(2,1)}, bf16[512,1,256]{2,0,1:T(8,128)(2,1)S(1)}, u32[]{:S(2)}, u32[]{:S(2)}) collective-permute-start(bf16[512,1,256]{2,0,1:T(8,128)(2,1)} %fusion.29), channel_id=1, source_target_pairs={{0,16},{1,17},{2,18},{3,19},{4,20},{5,21},{6,22},{7,23},{8,24},{9,... | collective-permute-start | bytes 786440 | tf_op jit(solution)/shard_map/ppermute | solution.py:16
where the time goes:
time: 79.7 us; the launch traced here: 79.3 us
  waiting for transfers between devices  38.1 us (48%)
  starting transfers between devices  25.2 us (32%)
  matrix products  6.69 us (8%)
  local copies, waits for them, and re-layouts  4.8 us (6%)
  other arithmetic  3.71 us (5%)
  between operations  0.81 us (1%)
    ppermute x4, waiting for transfers between devices, swapped(): return lax.ppermute(value, axis, pairs)  35.8 us
    ppermute x4, starting transfers between devices, swapped(): return lax.ppermute(value, axis, pairs)  19.5 us
    ppermute x2, starting transfers between devices, from_behind(): return lax.ppermute(value, axis, pairs)  5.69 us
    ppermute x2, waiting for transfers between devices, from_behind(): return lax.ppermute(value, axis, pairs)  2.32 us
    dot_general x1, matrix products, on_device(): jnp.einsum('tmep,ktmq->kmepq', hidden, stacked_grads, preferred_element_t...  1.93 us
    reshape x1, local copies, waits for them, and re-layouts  1.86 us
    convert_element_type x1, other arithmetic, on_device(): input_grads = (cotangent.astype(jnp.float32) + back_sum.reshape(tokens, m...  1.82 us
    convert_element_type x1, other arithmetic, on_device(): mixed = (inputs.astype(jnp.float32) + out_sum.reshape(tokens, model_local...  1.82 us
  transfers between devices with their start and end apart: 6, of which 5 were waited for; matrix products, arithmetic and copies ran while one was open for 10% of the time, Pallas kernels for 0%

commit v1 on v0

v1 whole, which is shorter than its diff:
```python
import functools

import jax
import jax.numpy as jnp
from jax import lax
from jax.experimental import pallas as pl
from jax.experimental.pallas import tpu as pltpu
from jax.sharding import PartitionSpec as P

MESH = pl.DeviceIdType.MESH
F32 = jnp.float32
BF16 = jnp.bfloat16
CHUNKS = 4
ROOT = 0.7978845608028654
CUBIC = 0.044715


def dot(a, b):
    return jnp.dot(a, b, preferred_element_type=F32)


def dot_nt(a, b):
    return lax.dot_general(a, b, (((1,), (1,)), ((), ())), preferred_element_type=F32)


def dot_tn(a, b):
    return lax.dot_general(a, b, (((0,), (0,)), ((), ())), preferred_element_type=F32)


def kernel(
    sections, far, expand,
    acts, emb, grads, loss, up, down,
    mixed, input_grads, up_grad, down_grad,
    x_own, x_far, g_own, g_far, u, v, hid, gpre, out_own, back_own,
    out_send, back_send, out_got, back_got, mixed_v, ingrad_v, upg_v, downg_v,
    send_sem, recv_sem, load_sem, store_sem, mix_sem,
):
    chunks, rows, width = x_own.shape
    section, tensor = lax.axis_index("section"), lax.axis_index("tensor")
    partner = tensor + far - 2 * far * (lax.rem(tensor // far, 2))
    first, last = section == 0, section == sections - 1

    def at(step, place):
        return {"section": section + step, "tensor": place}

    load_u = pltpu.make_async_copy(up, u, load_sem.at[0])
    load_v = pltpu.make_async_copy(down, v, load_sem.at[1])
    load_u.start()
    load_v.start()

    barrier = pltpu.get_barrier_semaphore()

    def greet(step, place):
        pl.semaphore_signal(barrier, inc=1, device_id=at(step, place), device_id_type=MESH)

    greet(0, partner)

    @pl.when(jnp.logical_not(last))
    def _():
        greet(1, partner)
        greet(1, tensor)

    @pl.when(jnp.logical_not(first))
    def _():
        greet(-1, partner)
        greet(-1, tensor)

    edge = jnp.logical_or(first, last)

    @pl.when(edge)
    def _():
        pl.semaphore_wait(barrier, 3)

    @pl.when(jnp.logical_not(edge))
    def _():
        pl.semaphore_wait(barrier, 5)

    def part(ref, c):
        return ref.at[pl.ds(pl.multiple_of(c * rows, rows), rows)]

    def copy(source, target, c, send, recv, step, place):
        return pltpu.make_async_remote_copy(
            src_ref=source,
            dst_ref=target.at[c],
            send_sem=send_sem.at[send, c],
            recv_sem=recv_sem.at[recv, c],
            device_id=at(step, place),
            device_id_type=MESH,
        )

    def acts_far(c):
        return copy(part(acts, c), x_far, c, 0, 0, 1, partner)

    def grads_far(c):
        return copy(part(grads, c), g_far, c, 1, 1, -1, partner)

    def acts_near(c):
        return copy(part(acts, c), x_own, c, 2, 2, 1, tensor)

    def grads_near(c):
        return copy(part(grads, c), g_own, c, 3, 3, -1, tensor)

    def emb_far(c):
        return copy(part(emb, c), x_far, c, 4, 0, 0, partner)

    def loss_far(c):
        return copy(part(loss, c), g_far, c, 4, 1, 0, partner)

    def emb_near(c):
        return pltpu.make_async_copy(part(emb, c), x_own.at[c], recv_sem.at[2, c])

    def loss_near(c):
        return pltpu.make_async_copy(part(loss, c), g_own.at[c], recv_sem.at[3, c])

    def out_copy(c):
        return copy(out_send.at[c], out_got, c, 5, 4, 0, partner)

    def back_copy(c):
        return copy(back_send.at[c], back_got, c, 6, 5, 0, partner)

    def start(c, carry):
        @pl.when(jnp.logical_not(last))
        def _():
            acts_far(c).start()
            acts_near(c).start()

        @pl.when(first)
        def _():
            emb_far(c).start()
            emb_near(c).start()

        @pl.when(jnp.logical_not(first))
        def _():
            grads_far(c).start()
            grads_near(c).start()

        @pl.when(last)
        def _():
            loss_far(c).start()
            loss_near(c).start()

        return carry

    lax.fori_loop(0, chunks, start, 0)
    load_u.wait()
    load_v.wait()

    def compute(c, carry):
        acts_far(c).wait_recv()
        acts_near(c).wait_recv()
        here = pl.ds(pl.multiple_of(c * rows, rows), rows)
        xo, xf = x_own[c], x_far[c]
        slopes = []
        out0 = xo.astype(F32)
        out1 = jnp.zeros((rows, width), F32)
        for j in range(expand):
            block = slice(j * width, (j + 1) * width)
            pre = dot(xo, u[0, :, block]) + dot(xf, u[1, :, block])
            square = pre * pre
            t = jnp.tanh(ROOT * (pre + CUBIC * (square * pre)))
            half = 0.5 * (1.0 + t)
            slopes.append(
                half + 0.5 * pre * (1.0 - t * t) * (ROOT * (1.0 + 3.0 * CUBIC * square))
            )
            h = (pre * half).astype(BF16)
            hid[here, block] = h
            out1 = out1 + dot(h, v[1, block, :])
            out0 = out0 + dot(h, v[0, block, :])
        out_send[c] = out1.astype(BF16)
        out_copy(c).start()
        out_own[c] = out0
        grads_far(c).wait_recv()
        grads_near(c).wait_recv()
        go, gf = g_own[c], g_far[c]
        back0 = go.astype(F32)
        back1 = jnp.zeros((rows, width), F32)
        for j in range(expand):
            block = slice(j * width, (j + 1) * width)
            gh = dot_nt(go, v[0, block, :]) + dot_nt(gf, v[1, block, :])
            gp = (gh * slopes[j]).astype(BF16)
            gpre[here, block] = gp
            back1 = back1 + dot_nt(gp, u[1, :, block])
            back0 = back0 + dot_nt(gp, u[0, :, block])
        back_send[c] = back1.astype(BF16)
        back_copy(c).start()
        back_own[c] = back0
        return carry

    lax.fori_loop(0, chunks, compute, 0)

    flat = (chunks * rows, width)
    for k, (xk, gk) in enumerate(((x_own, g_own), (x_far, g_far))):
        xs, gs = xk[...].reshape(flat), gk[...].reshape(flat)
        for j in range(expand):
            block = slice(j * width, (j + 1) * width)
            upg_v[k, :, block] = dot_tn(xs, gpre[:, block]).astype(BF16)
            downg_v[k, block, :] = dot_tn(hid[:, block], gs).astype(BF16)
    store_u = pltpu.make_async_copy(upg_v, up_grad, store_sem.at[0])
    store_d = pltpu.make_async_copy(downg_v, down_grad, store_sem.at[1])
    store_u.start()
    store_d.start()

    def store_mixed(c):
        return pltpu.make_async_copy(mixed_v.at[c], part(mixed, c), mix_sem.at[0, c])

    def store_ingrad(c):
        return pltpu.make_async_copy(ingrad_v.at[c], part(input_grads, c), mix_sem.at[1, c])

    def finish(c, carry):
        out_copy(c).wait_recv()
        mixed_v[c] = (out_own[c] + out_got[c].astype(F32)).astype(BF16)
        store_mixed(c).start()
        back_copy(c).wait_recv()
        ingrad_v[c] = (back_own[c] + back_got[c].astype(F32)).astype(BF16)
        store_ingrad(c).start()
        return carry

    lax.fori_loop(0, chunks, finish, 0)

    def drain(c, carry):
        out_copy(c).wait_send()
        back_copy(c).wait_send()

        @pl.when(jnp.logical_not(last))
        def _():
            acts_far(c).wait_send()
            acts_near(c).wait_send()

        @pl.when(first)
        def _():
            emb_far(c).wait_send()

        @pl.when(jnp.logical_not(first))
        def _():
            grads_far(c).wait_send()
            grads_near(c).wait_send()

        @pl.when(last)
        def _():
            loss_far(c).wait_send()

        store_mixed(c).wait()
        store_ingrad(c).wait()
        return carry

    lax.fori_loop(0, chunks, drain, 0)
    store_u.wait()
    store_d.wait()


def on_device(acts_prev, embedded, grads_next, loss_grad, up_weight, down_weight):
    sections, tensors = lax.axis_size("section"), lax.axis_size("tensor")
    tokens, width = acts_prev.shape
    up_local, down_local = up_weight[0], down_weight[0]
    factors, _, hidden = up_local.shape
    chunks, rows = CHUNKS, tokens // CHUNKS
    blocks = (chunks, rows, width)
    anywhere = pl.BlockSpec(memory_space=pl.ANY)

    def in_hbm(value):
        return pltpu.with_memory_space_constraint(value, pltpu.HBM)

    mixed, input_grads, up_grad, down_grad = pl.pallas_call(
        functools.partial(kernel, sections, tensors // 2, hidden // width),
        name="relay_layer",
        out_shape=(
            jax.ShapeDtypeStruct((tokens, width), BF16),
            jax.ShapeDtypeStruct((tokens, width), BF16),
            jax.ShapeDtypeStruct(up_local.shape, BF16),
            jax.ShapeDtypeStruct(down_local.shape, BF16),
        ),
        in_specs=[anywhere] * 6,
        out_specs=[anywhere] * 4,
        scratch_shapes=[
            pltpu.VMEM(blocks, BF16),
            pltpu.VMEM(blocks, BF16),
            pltpu.VMEM(blocks, BF16),
            pltpu.VMEM(blocks, BF16),
            pltpu.VMEM(up_local.shape, BF16),
            pltpu.VMEM(down_local.shape, BF16),
            pltpu.VMEM((tokens, hidden), BF16),
            pltpu.VMEM((tokens, hidden), BF16),
            pltpu.VMEM(blocks, F32),
            pltpu.VMEM(blocks, F32),
            pltpu.VMEM(blocks, BF16),
            pltpu.VMEM(blocks, BF16),
            pltpu.VMEM(blocks, BF16),
            pltpu.VMEM(blocks, BF16),
            pltpu.VMEM(blocks, BF16),
            pltpu.VMEM(blocks, BF16),
            pltpu.VMEM(up_local.shape, BF16),
            pltpu.VMEM(down_local.shape, BF16),
            pltpu.SemaphoreType.DMA((7, chunks)),
            pltpu.SemaphoreType.DMA((6, chunks)),
            pltpu.SemaphoreType.DMA((2,)),
            pltpu.SemaphoreType.DMA((2,)),
            pltpu.SemaphoreType.DMA((2, chunks)),
        ],
        compiler_params=pltpu.CompilerParams(
            collective_id=0, has_side_effects=True, vmem_limit_bytes=48 << 20
        ),
    )(*map(in_hbm, (acts_prev, embedded, grads_next, loss_grad, up_local, down_local)))
    return (mixed, input_grads, up_grad[None], down_grad[None])


def solution(mesh):
    in_specs = (
        P("section", "tensor"),
        P(None, "tensor"),
        P("section", "tensor"),
        P(None, "tensor"),
        P("section", None, None, "tensor"),
        P("section", None, "tensor", None),
    )
    out_specs = (
        P("section", "tensor"),
        P("section", "tensor"),
        P("section", None, None, "tensor"),
        P("section", None, "tensor", None),
    )
    return jax.shard_map(
        on_device, mesh=mesh, in_specs=in_specs, out_specs=out_specs, check_vma=False
    )
```

time: 79.7 us -> 62.3 us (0.78)
  the two profiles are of different devices: /device:TPU:196 before, /device:TPU:1 now
where the time goes in v1:
time: 62.3 us; the launch traced here: 62.1 us
  Pallas kernels  58.1 us (93%)
  local copies, waits for them, and re-layouts  3.35 us (5%)
  between operations  0.64 us (1%)
    pallas_call x1, Pallas kernels, on_device(): pl.pallas_call(functools.partial(kernel, sections, tensors // 2, hidden /...  58.1 us
    unnamed x4, local copies, waits for them, and re-layouts  3.35 us

profile of v1, /device:TPU:1, one launch (start us, length us, event | category | flops | bytes accessed | tf_op | source)
XLA Modules:
  0.0 62.1 jit_solution(5682383220699796426)
XLA Ops:
  0.6 58.1 %relay_layer.1 = (bf16[512,256]{1,0:T(8,128)(2,1)S(1)}, bf16[512,256]{1,0:T(8,128)(2,1)S(1)}, bf16[2,256,1024]{2,1,0:T(8,128)(2,1)S(1)}, bf16[2,1024,256]{2,1,0:T(8,128)(2,1)S(1)}) custom-call(bf16[512,256]{1,0:T(8,128)(2,1)} %acts.1, bf16[512,256]{1,0:T(8,128)(2,1)} %emb.1, bf16[512,256]{1,0:T(8,128)(2,1)} %grads.1, bf16[512,256]{1,0:T(8,128)(2,1)} %loss.1, ...), custom_call_target="tpu_custom_call" | custom-call | tf_op jit(solution)/shard_map/relay_layer/pallas_call | solution.py:263
  58.8 0.7 %copy.14 = bf16[512,256]{1,0:T(8,128)(2,1)} copy(bf16[512,256]{1,0:T(8,128)(2,1)S(1)} %get-tuple-element.16) | data formatting | bytes 524288
  59.5 0.7 %copy.15 = bf16[512,256]{1,0:T(8,128)(2,1)} copy(bf16[512,256]{1,0:T(8,128)(2,1)S(1)} %get-tuple-element.17) | data formatting | bytes 524288
  60.2 1.0 %copy.16 = bf16[1,2,256,1024]{3,2,1,0:T(8,128)(2,1)} copy(bf16[1,2,256,1024]{3,2,1,0:T(8,128)(2,1)S(1)} %bitcast.5) | data formatting | bytes 2097152
  61.2 1.0 %copy.17 = bf16[1,2,1024,256]{3,2,1,0:T(8,128)(2,1)} copy(bf16[1,2,1024,256]{3,2,1,0:T(8,128)(2,1)S(1)} %bitcast.4) | data formatting | bytes 2097152

commit v2 on v1

--- a/solution.py
+++ b/solution.py
@@ -32,8 +32,8 @@
     acts, emb, grads, loss, up, down,
     mixed, input_grads, up_grad, down_grad,
     x_own, x_far, g_own, g_far, u, v, hid, gpre, out_own, back_own,
-    out_send, back_send, out_got, back_got, mixed_v, ingrad_v, upg_v, downg_v,
-    send_sem, recv_sem, load_sem, store_sem, mix_sem,
+    out_send, back_send, out_got, back_got,
+    send_sem, recv_sem, load_sem, ready,
 ):
     chunks, rows, width = x_own.shape
     section, tensor = lax.axis_index("section"), lax.axis_index("tensor")
@@ -48,32 +48,49 @@
     load_u.start()
     load_v.start()
 
+    corner = jnp.logical_or(tensor == 0, tensor == far)
+    late = jnp.logical_and(first, tensor == 0)
+    hears_late = jnp.logical_and(
+        jnp.logical_and(section <= 1, corner), jnp.logical_not(late)
+    )
+    edge = jnp.logical_or(first, last)
     barrier = pltpu.get_barrier_semaphore()
 
-    def greet(step, place):
-        pl.semaphore_signal(barrier, inc=1, device_id=at(step, place), device_id_type=MESH)
-
-    greet(0, partner)
-
-    @pl.when(jnp.logical_not(last))
+    def tell(semaphore, step, place):
+        pl.semaphore_signal(
+            semaphore, inc=1, device_id=at(step, place), device_id_type=MESH
+        )
+
+    def tell_all(semaphore):
+        tell(semaphore, 0, partner)
+
+        @pl.when(jnp.logical_not(last))
+        def _():
+            tell(semaphore, 1, partner)
+            tell(semaphore, 1, tensor)
+
+        @pl.when(jnp.logical_not(first))
+        def _():
+            tell(semaphore, -1, partner)
+            tell(semaphore, -1, tensor)
+
+    def wait_for(peers, when):
+        @pl.when(when)
+        def _():
+            pl.semaphore_wait(barrier, peers)
+
+    pl.when(jnp.logical_not(late))(lambda: tell_all(barrier))
+    inner, prompt = jnp.logical_not(edge), jnp.logical_not(hears_late)
+    wait_for(5, jnp.logical_and(inner, prompt))
+    wait_for(4, jnp.logical_and(inner, hears_late))
+    wait_for(3, jnp.logical_and(edge, prompt))
+    wait_for(2, jnp.logical_and(edge, hears_late))
+
+    @pl.when(late)
     def _():
-        greet(1, partner)
-        greet(1, tensor)
-
-    @pl.when(jnp.logical_not(first))
-    def _():
-        greet(-1, partner)
-        greet(-1, tensor)
-
-    edge = jnp.logical_or(first, last)
-
-    @pl.when(edge)
-    def _():
-        pl.semaphore_wait(barrier, 3)
-
-    @pl.when(jnp.logical_not(edge))
-    def _():
-        pl.semaphore_wait(barrier, 5)
+        tell(ready, 0, partner)
+        tell(ready, 1, partner)
+        tell(ready, 1, tensor)
 
     def part(ref, c):
         return ref.at[pl.ds(pl.multiple_of(c * rows, rows), rows)]
@@ -118,6 +135,13 @@
     def back_copy(c):
         return copy(back_send.at[c], back_got, c, 6, 5, 0, partner)
 
+    def near_late(step, place):
+        return jnp.logical_and(section + step == 0, place == 0)
+
+    far_first = jnp.logical_and(first, jnp.logical_not(near_late(0, partner)))
+    down_far = jnp.logical_and(jnp.logical_not(first), jnp.logical_not(near_late(-1, partner)))
+    down_near = jnp.logical_and(jnp.logical_not(first), jnp.logical_not(near_late(-1, tensor)))
+
     def start(c, carry):
         @pl.when(jnp.logical_not(last))
         def _():
@@ -126,13 +150,11 @@
 
         @pl.when(first)
         def _():
-            emb_far(c).start()
             emb_near(c).start()
 
-        @pl.when(jnp.logical_not(first))
-        def _():
-            grads_far(c).start()
-            grads_near(c).start()
+        pl.when(far_first)(lambda: emb_far(c).start())
+        pl.when(down_far)(lambda: grads_far(c).start())
+        pl.when(down_near)(lambda: grads_near(c).start())
 
         @pl.when(last)
         def _():
@@ -141,7 +163,19 @@
 
         return carry
 
+    def start_late(c, carry):
+        pl.when(near_late(0, partner))(lambda: emb_far(c).start())
+        pl.when(near_late(-1, partner))(lambda: grads_far(c).start())
+        pl.when(near_late(-1, tensor))(lambda: grads_near(c).start())
+        return carry
+
     lax.fori_loop(0, chunks, start, 0)
+
+    @pl.when(hears_late)
+    def _():
+        pl.semaphore_wait(ready, 1)
+        lax.fori_loop(0, chunks, start_late, 0)
+
     load_u.wait()
     load_v.wait()
 
@@ -193,26 +227,14 @@
         xs, gs = xk[...].reshape(flat), gk[...].reshape(flat)
         for j in range(expand):
             block = slice(j * width, (j + 1) * width)
-            upg_v[k, :, block] = dot_tn(xs, gpre[:, block]).astype(BF16)
-            downg_v[k, block, :] = dot_tn(hid[:, block], gs).astype(BF16)
-    store_u = pltpu.make_async_copy(upg_v, up_grad, store_sem.at[0])
-    store_d = pltpu.make_async_copy(downg_v, down_grad, store_sem.at[1])
-    store_u.start()
-    store_d.start()
-
-    def store_mixed(c):
-        return pltpu.make_async_copy(mixed_v.at[c], part(mixed, c), mix_sem.at[0, c])
-
-    def store_ingrad(c):
-        return pltpu.make_async_copy(ingrad_v.at[c], part(input_grads, c), mix_sem.at[1, c])
-
+            up_grad[k, :, block] = dot_tn(xs, gpre[:, block]).astype(BF16)
+            down_grad[k, block, :] = dot_tn(hid[:, block], gs).astype(BF16)
     def finish(c, carry):
         out_copy(c).wait_recv()
-        mixed_v[c] = (out_own[c] + out_got[c].astype(F32)).astype(BF16)
-        store_mixed(c).start()
+        here = pl.ds(pl.multiple_of(c * rows, rows), rows)
+        mixed[here] = (out_own[c] + out_got[c].astype(F32)).astype(BF16)
         back_copy(c).wait_recv()
-        ingrad_v[c] = (back_own[c] + back_got[c].astype(F32)).astype(BF16)
-        store_ingrad(c).start()
+        input_grads[here] = (back_own[c] + back_got[c].astype(F32)).astype(BF16)
         return carry
 
     lax.fori_loop(0, chunks, finish, 0)
@@ -239,13 +261,21 @@
         def _():
             loss_far(c).wait_send()
 
-        store_mixed(c).wait()
-        store_ingrad(c).wait()
         return carry
 
     lax.fori_loop(0, chunks, drain, 0)
-    store_u.wait()
-    store_d.wait()
+
+
+def flush(*refs):
+    done = refs[-1]
+    count = done.shape[0]
+    copies = [
+        pltpu.make_async_copy(refs[i], refs[count + i], done.at[i]) for i in range(count)
+    ]
+    for copy in copies:
+        copy.start()
+    for copy in copies:
+        copy.wait()
 
 
 def on_device(acts_prev, embedded, grads_next, loss_grad, up_weight, down_weight):
@@ -260,17 +290,13 @@
     def in_hbm(value):
         return pltpu.with_memory_space_constraint(value, pltpu.HBM)
 
-    mixed, input_grads, up_grad, down_grad = pl.pallas_call(
+    shapes = (acts_prev.shape, acts_prev.shape, up_local.shape, down_local.shape)
+    results = pl.pallas_call(
         functools.partial(kernel, sections, tensors // 2, hidden // width),
         name="relay_layer",
-        out_shape=(
-            jax.ShapeDtypeStruct((tokens, width), BF16),
-            jax.ShapeDtypeStruct((tokens, width), BF16),
-            jax.ShapeDtypeStruct(up_local.shape, BF16),
-            jax.ShapeDtypeStruct(down_local.shape, BF16),
-        ),
+        out_shape=tuple(pltpu.VMEM(shape, BF16) for shape in shapes),
         in_specs=[anywhere] * 6,
-        out_specs=[anywhere] * 4,
+        out_specs=[pl.BlockSpec(memory_space=pltpu.VMEM)] * 4,
         scratch_shapes=[
             pltpu.VMEM(blocks, BF16),
             pltpu.VMEM(blocks, BF16),
@@ -286,20 +312,24 @@
             pltpu.VMEM(blocks, BF16),
             pltpu.VMEM(blocks, BF16),
             pltpu.VMEM(blocks, BF16),
-            pltpu.VMEM(blocks, BF16),
-            pltpu.VMEM(blocks, BF16),
-            pltpu.VMEM(up_local.shape, BF16),
-            pltpu.VMEM(down_local.shape, BF16),
             pltpu.SemaphoreType.DMA((7, chunks)),
             pltpu.SemaphoreType.DMA((6, chunks)),
             pltpu.SemaphoreType.DMA((2,)),
-            pltpu.SemaphoreType.DMA((2,)),
-            pltpu.SemaphoreType.DMA((2, chunks)),
+            pltpu.SemaphoreType.REGULAR,
         ],
         compiler_params=pltpu.CompilerParams(
             collective_id=0, has_side_effects=True, vmem_limit_bytes=48 << 20
         ),
     )(*map(in_hbm, (acts_prev, embedded, grads_next, loss_grad, up_local, down_local)))
+    mixed, input_grads, up_grad, down_grad = pl.pallas_call(
+        flush,
+        name="flush",
+        out_shape=tuple(pltpu.HBM(shape, BF16) for shape in shapes),
+        in_specs=[anywhere] * 4,
+        out_specs=[anywhere] * 4,
+        scratch_shapes=[pltpu.SemaphoreType.DMA((4,))],
+        compiler_params=pltpu.CompilerParams(vmem_limit_bytes=1 << 20),
+    )(*results)
     return (mixed, input_grads, up_grad[None], down_grad[None])
 
 

time: 62.3 us -> 56.9 us (0.913)
  local copies, waits for them, and re-layouts: 3.35 us -> 0 us
  Pallas kernels: 58.1 us -> 56.1 us
    pallas_call x1, Pallas kernels: 58.1 us -> 54.6 us  [on_device(): pl.pallas_call(functools.partial(kernel, sections, tensors // 2, hidden /...]
    unnamed x4 -> x0, local copies, waits for them, and re-layouts: 3.35 us -> none
    pallas_call x0 -> x1, Pallas kernels: none -> 1.53 us  [on_device(): pl.pallas_call(flush, name='flush', out_shape=tuple((pltpu.HBM(shape, BF1...]
where the time goes in v2:
time: 56.9 us; the launch traced here: 56.7 us
  Pallas kernels  56.1 us (99%)
  between operations  0.64 us (1%)
    pallas_call x1, Pallas kernels, on_device(): pl.pallas_call(functools.partial(kernel, sections, tensors // 2, hidden /...  54.6 us
    pallas_call x1, Pallas kernels, on_device(): pl.pallas_call(flush, name='flush', out_shape=tuple((pltpu.HBM(shape, BF1...  1.53 us

profile of v2, /device:TPU:1, one launch (start us, length us, event | category | flops | bytes accessed | tf_op | source)
XLA Modules:
  0.0 56.7 jit_solution(16692040671305738564)
XLA Ops:
  0.6 54.6 %relay_layer.1 = (bf16[512,256]{1,0:T(8,128)(2,1)S(1)}, bf16[512,256]{1,0:T(8,128)(2,1)S(1)}, bf16[2,256,1024]{2,1,0:T(8,128)(2,1)S(1)}, bf16[2,1024,256]{2,1,0:T(8,128)(2,1)S(1)}) custom-call(bf16[512,256]{1,0:T(8,128)(2,1)} %acts.1, bf16[512,256]{1,0:T(8,128)(2,1)} %emb.1, bf16[512,256]{1,0:T(8,128)(2,1)} %grads.1, bf16[512,256]{1,0:T(8,128)(2,1)} %loss.1, ...), custom_call_target="tpu_custom_call" | custom-call | tf_op jit(solution)/shard_map/relay_layer/pallas_call | solution.py:294
  55.2 1.5 %flush.1 = (bf16[512,256]{1,0:T(8,128)(2,1)}, bf16[512,256]{1,0:T(8,128)(2,1)}, bf16[2,256,1024]{2,1,0:T(8,128)(2,1)}, bf16[2,1024,256]{2,1,0:T(8,128)(2,1)}) custom-call(bf16[512,256]{1,0:T(8,128)(2,1)S(1)} %get-tuple-element.12.refs_0_, bf16[512,256]{1,0:T(8,128)(2,1)S(1)} %get-tuple-element.13.refs_1_, ...), custom_call_target="tpu_custom_call" | custom-call | tf_op jit(solution)/shard_map/flush/pallas_call | solution.py:324

commit v3 on v2

--- a/solution.py
+++ b/solution.py
@@ -10,7 +10,7 @@
 MESH = pl.DeviceIdType.MESH
 F32 = jnp.float32
 BF16 = jnp.bfloat16
-CHUNKS = 4
+CHUNKS = 2
 ROOT = 0.7978845608028654
 CUBIC = 0.044715
 
@@ -33,7 +33,7 @@
     mixed, input_grads, up_grad, down_grad,
     x_own, x_far, g_own, g_far, u, v, hid, gpre, out_own, back_own,
     out_send, back_send, out_got, back_got,
-    send_sem, recv_sem, load_sem, ready,
+    send_sem, recv_sem, load_sem, ready, upper_in,
 ):
     chunks, rows, width = x_own.shape
     section, tensor = lax.axis_index("section"), lax.axis_index("tensor")
@@ -45,15 +45,12 @@
 
     load_u = pltpu.make_async_copy(up, u, load_sem.at[0])
     load_v = pltpu.make_async_copy(down, v, load_sem.at[1])
-    load_u.start()
-    load_v.start()
 
     corner = jnp.logical_or(tensor == 0, tensor == far)
     late = jnp.logical_and(first, tensor == 0)
     hears_late = jnp.logical_and(
         jnp.logical_and(section <= 1, corner), jnp.logical_not(late)
     )
-    edge = jnp.logical_or(first, last)
     barrier = pltpu.get_barrier_semaphore()
 
     def tell(semaphore, step, place):
@@ -61,36 +58,38 @@
             semaphore, inc=1, device_id=at(step, place), device_id_type=MESH
         )
 
-    def tell_all(semaphore):
-        tell(semaphore, 0, partner)
-
-        @pl.when(jnp.logical_not(last))
-        def _():
-            tell(semaphore, 1, partner)
-            tell(semaphore, 1, tensor)
-
-        @pl.when(jnp.logical_not(first))
-        def _():
-            tell(semaphore, -1, partner)
-            tell(semaphore, -1, tensor)
+    even = lax.rem(section, 2) == 0
+    odd = jnp.logical_not(even)
+    other = 1 - 2 * lax.rem(section, 2)
+    has_upper = jnp.logical_and(odd, jnp.logical_not(last))
+    has_lower = jnp.logical_and(even, jnp.logical_not(first))
+
+    @pl.when(jnp.logical_not(late))
+    def _():
+        tell(barrier, 0, partner)
+        tell(barrier, other, partner)
+        tell(barrier, other, tensor)
+
+        pl.when(has_upper)(lambda: tell(barrier, 1, tensor))
+
+    load_u.start()
+    load_v.start()
 
     def wait_for(peers, when):
         @pl.when(when)
         def _():
             pl.semaphore_wait(barrier, peers)
 
-    pl.when(jnp.logical_not(late))(lambda: tell_all(barrier))
-    inner, prompt = jnp.logical_not(edge), jnp.logical_not(hears_late)
-    wait_for(5, jnp.logical_and(inner, prompt))
-    wait_for(4, jnp.logical_and(inner, hears_late))
-    wait_for(3, jnp.logical_and(edge, prompt))
-    wait_for(2, jnp.logical_and(edge, hears_late))
+    wait_for(4, has_lower)
+    wait_for(3, jnp.logical_and(jnp.logical_not(has_lower), jnp.logical_not(hears_late)))
+    wait_for(2, hears_late)
 
     @pl.when(late)
     def _():
         tell(ready, 0, partner)
-        tell(ready, 1, partner)
         tell(ready, 1, tensor)
+
+    pl.when(has_lower)(lambda: tell(upper_in, -1, tensor))
 
     def part(ref, c):
         return ref.at[pl.ds(pl.multiple_of(c * rows, rows), rows)]
@@ -123,6 +122,15 @@
     def loss_far(c):
         return copy(part(loss, c), g_far, c, 4, 1, 0, partner)
 
+    def pass_acts(c):
+        return copy(x_own.at[c], x_far, c, 4, 0, 0, partner)
+
+    def pass_grads(c):
+        return copy(g_own.at[c], g_far, c, 4, 1, 0, partner)
+
+    def pass_late(c):
+        return copy(g_own.at[c], g_far, c, 1, 1, 0, partner)
+
     def emb_near(c):
         return pltpu.make_async_copy(part(emb, c), x_own.at[c], recv_sem.at[2, c])
 
@@ -138,50 +146,61 @@
     def near_late(step, place):
         return jnp.logical_and(section + step == 0, place == 0)
 
-    far_first = jnp.logical_and(first, jnp.logical_not(near_late(0, partner)))
-    down_far = jnp.logical_and(jnp.logical_not(first), jnp.logical_not(near_late(-1, partner)))
-    down_near = jnp.logical_and(jnp.logical_not(first), jnp.logical_not(near_late(-1, tensor)))
-
-    def start(c, carry):
-        @pl.when(jnp.logical_not(last))
-        def _():
-            acts_far(c).start()
-            acts_near(c).start()
-
-        @pl.when(first)
-        def _():
-            emb_near(c).start()
-
+    beside_late, across_late = near_late(0, partner), near_late(-1, partner)
+    far_first = jnp.logical_and(first, jnp.logical_not(beside_late))
+    odd_far = jnp.logical_and(odd, jnp.logical_not(across_late))
+    odd_near = jnp.logical_and(odd, jnp.logical_not(near_late(-1, tensor)))
+
+    def start_far(c, carry):
+        pl.when(even)(lambda: acts_far(c).start())
+        pl.when(odd_far)(lambda: grads_far(c).start())
         pl.when(far_first)(lambda: emb_far(c).start())
-        pl.when(down_far)(lambda: grads_far(c).start())
-        pl.when(down_near)(lambda: grads_near(c).start())
-
-        @pl.when(last)
-        def _():
-            loss_far(c).start()
-            loss_near(c).start()
-
+        pl.when(last)(lambda: loss_far(c).start())
+        return carry
+
+    def start_near(c, carry):
+        pl.when(even)(lambda: acts_near(c).start())
+        pl.when(jnp.logical_or(odd_near, has_lower))(lambda: grads_near(c).start())
+        pl.when(first)(lambda: emb_near(c).start())
+        pl.when(last)(lambda: loss_near(c).start())
+        return carry
+
+    def start_upper(c, carry):
+        acts_near(c).start()
         return carry
 
     def start_late(c, carry):
-        pl.when(near_late(0, partner))(lambda: emb_far(c).start())
-        pl.when(near_late(-1, partner))(lambda: grads_far(c).start())
+        pl.when(beside_late)(lambda: emb_far(c).start())
         pl.when(near_late(-1, tensor))(lambda: grads_near(c).start())
         return carry
 
-    lax.fori_loop(0, chunks, start, 0)
-
-    @pl.when(hears_late)
+    def pass_on(c, carry):
+        acts_near(c).wait_recv()
+        grads_near(c).wait_recv()
+        pl.when(has_lower)(lambda: pass_acts(c).start())
+        pl.when(has_upper)(lambda: pass_grads(c).start())
+        pl.when(beside_late)(lambda: pass_late(c).start())
+        return carry
+
+    lax.fori_loop(0, chunks, start_near, 0)
+    lax.fori_loop(0, chunks, start_far, 0)
+
+    @pl.when(has_upper)
+    def _():
+        pl.semaphore_wait(upper_in, 1)
+        lax.fori_loop(0, chunks, start_upper, 0)
+
+    @pl.when(jnp.logical_and(hears_late, jnp.logical_not(across_late)))
     def _():
         pl.semaphore_wait(ready, 1)
         lax.fori_loop(0, chunks, start_late, 0)
 
+    lax.fori_loop(0, chunks, pass_on, 0)
     load_u.wait()
     load_v.wait()
 
     def compute(c, carry):
         acts_far(c).wait_recv()
-        acts_near(c).wait_recv()
         here = pl.ds(pl.multiple_of(c * rows, rows), rows)
         xo, xf = x_own[c], x_far[c]
         slopes = []
@@ -204,7 +223,6 @@
         out_copy(c).start()
         out_own[c] = out0
         grads_far(c).wait_recv()
-        grads_near(c).wait_recv()
         go, gf = g_own[c], g_far[c]
         back0 = go.astype(F32)
         back1 = jnp.zeros((rows, width), F32)
@@ -229,41 +247,27 @@
             block = slice(j * width, (j + 1) * width)
             up_grad[k, :, block] = dot_tn(xs, gpre[:, block]).astype(BF16)
             down_grad[k, block, :] = dot_tn(hid[:, block], gs).astype(BF16)
+    def drain(c, carry):
+        emb_far(c).wait_send()
+        pl.when(even)(lambda: acts_far(c).wait_send())
+        pl.when(jnp.logical_or(odd_far, beside_late))(lambda: grads_far(c).wait_send())
+        pl.when(jnp.logical_not(last))(lambda: acts_near(c).wait_send())
+        pl.when(jnp.logical_not(first))(lambda: grads_near(c).wait_send())
+        return carry
+
+    lax.fori_loop(0, chunks, drain, 0)
+
     def finish(c, carry):
         out_copy(c).wait_recv()
         here = pl.ds(pl.multiple_of(c * rows, rows), rows)
         mixed[here] = (out_own[c] + out_got[c].astype(F32)).astype(BF16)
         back_copy(c).wait_recv()
         input_grads[here] = (back_own[c] + back_got[c].astype(F32)).astype(BF16)
-        return carry
-
-    lax.fori_loop(0, chunks, finish, 0)
-
-    def drain(c, carry):
         out_copy(c).wait_send()
         back_copy(c).wait_send()
-
-        @pl.when(jnp.logical_not(last))
-        def _():
-            acts_far(c).wait_send()
-            acts_near(c).wait_send()
-
-        @pl.when(first)
-        def _():
-            emb_far(c).wait_send()
-
-        @pl.when(jnp.logical_not(first))
-        def _():
-            grads_far(c).wait_send()
-            grads_near(c).wait_send()
-
-        @pl.when(last)
-        def _():
-            loss_far(c).wait_send()
-
-        return carry
-
-    lax.fori_loop(0, chunks, drain, 0)
+        return carry
+
+    lax.fori_loop(0, chunks, finish, 0)
 
 
 def flush(*refs):
@@ -315,6 +319,7 @@
             pltpu.SemaphoreType.DMA((7, chunks)),
             pltpu.SemaphoreType.DMA((6, chunks)),
             pltpu.SemaphoreType.DMA((2,)),
+            pltpu.SemaphoreType.REGULAR,
             pltpu.SemaphoreType.REGULAR,
         ],
         compiler_params=pltpu.CompilerParams(

time: 56.9 us -> 55.8 us (0.981)
  the two profiles are of different devices: /device:TPU:1 before, /device:TPU:16 now
where the time goes in v3:
time: 55.8 us; the launch traced here: 55.7 us
  Pallas kernels  55 us (99%)
  between operations  0.64 us (1%)
    pallas_call x1, Pallas kernels, on_device(): pl.pallas_call(functools.partial(kernel, sections, tensors // 2, hidden /...  53.5 us
    pallas_call x1, Pallas kernels, on_device(): pl.pallas_call(flush, name='flush', out_shape=tuple((pltpu.HBM(shape, BF1...  1.53 us

profile of v3, /device:TPU:16, one launch (start us, length us, event | category | flops | bytes accessed | tf_op | source)
XLA Modules:
  0.0 55.7 jit_solution(11796425263495109976)
XLA Ops:
  0.6 53.5 %relay_layer.1 = (bf16[512,256]{1,0:T(8,128)(2,1)S(1)}, bf16[512,256]{1,0:T(8,128)(2,1)S(1)}, bf16[2,256,1024]{2,1,0:T(8,128)(2,1)S(1)}, bf16[2,1024,256]{2,1,0:T(8,128)(2,1)S(1)}) custom-call(bf16[512,256]{1,0:T(8,128)(2,1)} %acts.1, bf16[512,256]{1,0:T(8,128)(2,1)} %emb.1, bf16[512,256]{1,0:T(8,128)(2,1)} %grads.1, bf16[512,256]{1,0:T(8,128)(2,1)} %loss.1, ...), custom_call_target="tpu_custom_call" | custom-call | tf_op jit(solution)/shard_map/relay_layer/pallas_call | solution.py:298
  54.2 1.5 %flush.1 = (bf16[512,256]{1,0:T(8,128)(2,1)}, bf16[512,256]{1,0:T(8,128)(2,1)}, bf16[2,256,1024]{2,1,0:T(8,128)(2,1)}, bf16[2,1024,256]{2,1,0:T(8,128)(2,1)}) custom-call(bf16[512,256]{1,0:T(8,128)(2,1)S(1)} %get-tuple-element.12.refs_0_, bf16[512,256]{1,0:T(8,128)(2,1)S(1)} %get-tuple-element.13.refs_1_, ...), custom_call_target="tpu_custom_call" | custom-call | tf_op jit(solution)/shard_map/flush/pallas_call | solution.py:329

commit v4 on v3

--- a/solution.py
+++ b/solution.py
@@ -183,7 +183,8 @@
         return carry
 
     lax.fori_loop(0, chunks, start_near, 0)
-    lax.fori_loop(0, chunks, start_far, 0)
+    early = jnp.where(has_lower, chunks - 1, chunks)
+    lax.fori_loop(0, early, start_far, 0)
 
     @pl.when(has_upper)
     def _():
@@ -196,6 +197,7 @@
         lax.fori_loop(0, chunks, start_late, 0)
 
     lax.fori_loop(0, chunks, pass_on, 0)
+    lax.fori_loop(early, chunks, start_far, 0)
     load_u.wait()
     load_v.wait()
 
@@ -247,6 +249,7 @@
             block = slice(j * width, (j + 1) * width)
             up_grad[k, :, block] = dot_tn(xs, gpre[:, block]).astype(BF16)
             down_grad[k, block, :] = dot_tn(hid[:, block], gs).astype(BF16)
+
     def drain(c, carry):
         emb_far(c).wait_send()
         pl.when(even)(lambda: acts_far(c).wait_send())

time: 55.8 us -> 55.8 us (level)
  no operation moved by 1% of the time
where the time goes in v4:
time: 55.8 us; the launch traced here: 55.7 us
  Pallas kernels  55 us (99%)
  between operations  0.64 us (1%)
    pallas_call x1, Pallas kernels, on_device(): pl.pallas_call(functools.partial(kernel, sections, tensors // 2, hidden /...  53.5 us
    pallas_call x1, Pallas kernels, on_device(): pl.pallas_call(flush, name='flush', out_shape=tuple((pltpu.HBM(shape, BF1...  1.53 us

profile of v4, /device:TPU:16, one launch (start us, length us, event | category | flops | bytes accessed | tf_op | source)
XLA Modules:
  0.0 55.7 jit_solution(5224507032643110497)
XLA Ops:
  0.6 53.5 %relay_layer.1 = (bf16[512,256]{1,0:T(8,128)(2,1)S(1)}, bf16[512,256]{1,0:T(8,128)(2,1)S(1)}, bf16[2,256,1024]{2,1,0:T(8,128)(2,1)S(1)}, bf16[2,1024,256]{2,1,0:T(8,128)(2,1)S(1)}) custom-call(bf16[512,256]{1,0:T(8,128)(2,1)} %acts.1, bf16[512,256]{1,0:T(8,128)(2,1)} %emb.1, bf16[512,256]{1,0:T(8,128)(2,1)} %grads.1, bf16[512,256]{1,0:T(8,128)(2,1)} %loss.1, ...), custom_call_target="tpu_custom_call" | custom-call | tf_op jit(solution)/shard_map/relay_layer/pallas_call | solution.py:301
  54.2 1.5 %flush.1 = (bf16[512,256]{1,0:T(8,128)(2,1)}, bf16[512,256]{1,0:T(8,128)(2,1)}, bf16[2,256,1024]{2,1,0:T(8,128)(2,1)}, bf16[2,1024,256]{2,1,0:T(8,128)(2,1)}) custom-call(bf16[512,256]{1,0:T(8,128)(2,1)S(1)} %get-tuple-element.12.refs_0_, bf16[512,256]{1,0:T(8,128)(2,1)S(1)} %get-tuple-element.13.refs_1_, ...), custom_call_target="tpu_custom_call" | custom-call | tf_op jit(solution)/shard_map/flush/pallas_call | solution.py:332

commit v5 on v4

--- a/solution.py
+++ b/solution.py
@@ -131,6 +131,9 @@
     def pass_late(c):
         return copy(g_own.at[c], g_far, c, 1, 1, 0, partner)
 
+    def wait_for_block(target, recv, c):
+        copy(target.at[c], target, c, 0, recv, 0, partner).wait_recv()
+
     def emb_near(c):
         return pltpu.make_async_copy(part(emb, c), x_own.at[c], recv_sem.at[2, c])
 
@@ -175,8 +178,8 @@
         return carry
 
     def pass_on(c, carry):
-        acts_near(c).wait_recv()
-        grads_near(c).wait_recv()
+        wait_for_block(x_own, 2, c)
+        wait_for_block(g_own, 3, c)
         pl.when(has_lower)(lambda: pass_acts(c).start())
         pl.when(has_upper)(lambda: pass_grads(c).start())
         pl.when(beside_late)(lambda: pass_late(c).start())
@@ -202,7 +205,7 @@
     load_v.wait()
 
     def compute(c, carry):
-        acts_far(c).wait_recv()
+        wait_for_block(x_far, 0, c)
         here = pl.ds(pl.multiple_of(c * rows, rows), rows)
         xo, xf = x_own[c], x_far[c]
         slopes = []
@@ -224,7 +227,7 @@
         out_send[c] = out1.astype(BF16)
         out_copy(c).start()
         out_own[c] = out0
-        grads_far(c).wait_recv()
+        wait_for_block(g_far, 1, c)
         go, gf = g_own[c], g_far[c]
         back0 = go.astype(F32)
         back1 = jnp.zeros((rows, width), F32)
@@ -253,7 +256,8 @@
     def drain(c, carry):
         emb_far(c).wait_send()
         pl.when(even)(lambda: acts_far(c).wait_send())
-        pl.when(jnp.logical_or(odd_far, beside_late))(lambda: grads_far(c).wait_send())
+        pl.when(odd_far)(lambda: grads_far(c).wait_send())
+        pl.when(beside_late)(lambda: pass_late(c).wait_send())
         pl.when(jnp.logical_not(last))(lambda: acts_near(c).wait_send())
         pl.when(jnp.logical_not(first))(lambda: grads_near(c).wait_send())
         return carry

time: 55.8 us -> 55.8 us (level)
  no operation moved by 1% of the time
where the time goes in v5:
time: 55.8 us; the launch traced here: 55.7 us
  Pallas kernels  55 us (99%)
  between operations  0.64 us (1%)
    pallas_call x1, Pallas kernels, on_device(): pl.pallas_call(functools.partial(kernel, sections, tensors // 2, hidden /...  53.5 us
    pallas_call x1, Pallas kernels, on_device(): pl.pallas_call(flush, name='flush', out_shape=tuple((pltpu.HBM(shape, BF1...  1.53 us

profile of v5, /device:TPU:16, one launch (start us, length us, event | category | flops | bytes accessed | tf_op | source)
XLA Modules:
  0.0 55.7 jit_solution(9366316426054559389)
XLA Ops:
  0.6 53.5 %relay_layer.1 = (bf16[512,256]{1,0:T(8,128)(2,1)S(1)}, bf16[512,256]{1,0:T(8,128)(2,1)S(1)}, bf16[2,256,1024]{2,1,0:T(8,128)(2,1)S(1)}, bf16[2,1024,256]{2,1,0:T(8,128)(2,1)S(1)}) custom-call(bf16[512,256]{1,0:T(8,128)(2,1)} %acts.1, bf16[512,256]{1,0:T(8,128)(2,1)} %emb.1, bf16[512,256]{1,0:T(8,128)(2,1)} %grads.1, bf16[512,256]{1,0:T(8,128)(2,1)} %loss.1, ...), custom_call_target="tpu_custom_call" | custom-call | tf_op jit(solution)/shard_map/relay_layer/pallas_call | solution.py:305
  54.2 1.5 %flush.1 = (bf16[512,256]{1,0:T(8,128)(2,1)}, bf16[512,256]{1,0:T(8,128)(2,1)}, bf16[2,256,1024]{2,1,0:T(8,128)(2,1)}, bf16[2,1024,256]{2,1,0:T(8,128)(2,1)}) custom-call(bf16[512,256]{1,0:T(8,128)(2,1)S(1)} %get-tuple-element.12.refs_0_, bf16[512,256]{1,0:T(8,128)(2,1)S(1)} %get-tuple-element.13.refs_1_, ...), custom_call_target="tpu_custom_call" | custom-call | tf_op jit(solution)/shard_map/flush/pallas_call | solution.py:336

commit v6 on v5

--- a/solution.py
+++ b/solution.py
@@ -185,9 +185,9 @@
         pl.when(beside_late)(lambda: pass_late(c).start())
         return carry
 
-    lax.fori_loop(0, chunks, start_near, 0)
     early = jnp.where(has_lower, chunks - 1, chunks)
     lax.fori_loop(0, early, start_far, 0)
+    lax.fori_loop(0, chunks, start_near, 0)
 
     @pl.when(has_upper)
     def _():

time: 55.8 us -> 55.7 us (level)
  no operation moved by 1% of the time
where the time goes in v6:
time: 55.7 us; the launch traced here: 55.6 us
  Pallas kernels  54.9 us (99%)
  between operations  0.64 us (1%)
    pallas_call x1, Pallas kernels, on_device(): pl.pallas_call(functools.partial(kernel, sections, tensors // 2, hidden /...  53.4 us
    pallas_call x1, Pallas kernels, on_device(): pl.pallas_call(flush, name='flush', out_shape=tuple((pltpu.HBM(shape, BF1...  1.53 us

profile of v6, /device:TPU:16, one launch (start us, length us, event | category | flops | bytes accessed | tf_op | source)
XLA Modules:
  0.0 55.6 jit_solution(6197896225425207735)
XLA Ops:
  0.6 53.4 %relay_layer.1 = (bf16[512,256]{1,0:T(8,128)(2,1)S(1)}, bf16[512,256]{1,0:T(8,128)(2,1)S(1)}, bf16[2,256,1024]{2,1,0:T(8,128)(2,1)S(1)}, bf16[2,1024,256]{2,1,0:T(8,128)(2,1)S(1)}) custom-call(bf16[512,256]{1,0:T(8,128)(2,1)} %acts.1, bf16[512,256]{1,0:T(8,128)(2,1)} %emb.1, bf16[512,256]{1,0:T(8,128)(2,1)} %grads.1, bf16[512,256]{1,0:T(8,128)(2,1)} %loss.1, ...), custom_call_target="tpu_custom_call" | custom-call | tf_op jit(solution)/shard_map/relay_layer/pallas_call | solution.py:305
  54.1 1.5 %flush.1 = (bf16[512,256]{1,0:T(8,128)(2,1)}, bf16[512,256]{1,0:T(8,128)(2,1)}, bf16[2,256,1024]{2,1,0:T(8,128)(2,1)}, bf16[2,1024,256]{2,1,0:T(8,128)(2,1)}) custom-call(bf16[512,256]{1,0:T(8,128)(2,1)S(1)} %get-tuple-element.12.refs_0_, bf16[512,256]{1,0:T(8,128)(2,1)S(1)} %get-tuple-element.13.refs_1_, ...), custom_call_target="tpu_custom_call" | custom-call | tf_op jit(solution)/shard_map/flush/pallas_call | solution.py:336
